TPU v7x, 32 devices: a whole 2x2x4 slice. The times are simulated.
32 devices in a mesh: pipe: 4 (over y, core), expert: 8 (over z, x).
Axes of the slice: x: 2, y: 2, z: 4, core: 2. Of those that a mesh axis runs over, the one named last changes fastest.
Arguments:
- tokens: bfloat16 [4, 1024, 2048], P('pipe', 'expert'), may hold values from -6 to 6
- out_grad: bfloat16 [4, 1024, 2048], P('pipe', 'expert'), may hold values from -6 to 6
- gates: float32 [4, 1024, 2], P('pipe', 'expert'), may hold values from 0.1 to 1
- expert_ids: int32 [4, 1024, 2], P('pipe', 'expert'), may hold values from 0 to 7, all different within a row; in each aligned block of 128 rows (0 to 127, 128 to 255, ..., all dimensions but the last counted through in order) at most 64 rows name the same one
- w_gate: bfloat16 [4, 8, 2048, 768], P('pipe', 'expert'), may hold values from -0.125 to 0.125
- w_up: bfloat16 [4, 8, 2048, 768], P('pipe', 'expert'), may hold values from -0.125 to 0.125
- w_down: bfloat16 [4, 8, 768, 2048], P('pipe', 'expert'), may hold values from -0.21875 to 0.21875
Outputs:
- arrived: bfloat16 [4, 1024, 2048], P('pipe', 'expert')
- grad_gates: bfloat16 [4, 1024, 2], P('pipe', 'expert')
Inputs may be any that keep to these rules, and one draw needn't show every extreme that they name: `expert_ids`: the 2 ids of a token differ. In each aligned block of 128 rows of a section (the tokens of one device) no expert is named by more than 64 rows, a bound that some block reaches.
All inputs are finite; a program needn't handle non-finite values.
Results may differ from a plain program's by a relative error of at most 0.0057.
Values may be sent and summed in bfloat16 or wider, within the bound.
A program may use at most 64 MiB of HBM per device.

v0:
```python
import jax
import jax.numpy as jnp
from jax import lax
from jax.sharding import PartitionSpec as P


def passed_along(value, axis, steps):
    count = lax.axis_size(axis)
    leading, last = (max(0, -steps), min(count, count - steps))
    return lax.ppermute(value, axis, [(source, source + steps) for source in range(leading, last)])


def forward_part(slot_tokens, gate_weight, up_weight):
    sources, count, width = slot_tokens.shape
    rows = slot_tokens.reshape(sources * count, width)
    gate = jnp.dot(rows, gate_weight, preferred_element_type=jnp.float32)
    up_proj = jnp.dot(rows, up_weight, preferred_element_type=jnp.float32)
    hidden_units = gate.shape[1]
    return (
        gate.reshape(sources, count, hidden_units),
        up_proj.reshape(sources, count, hidden_units),
    )


def down_part(slot_grads, down_weight):
    sources, count, width = slot_grads.shape
    row_grads = slot_grads.reshape(sources * count, width)
    contract_last = (((1,), (1,)), ((), ()))
    d_hidden = lax.dot_general(
        row_grads, down_weight, contract_last, preferred_element_type=jnp.float32
    )
    return d_hidden.reshape(sources, count, d_hidden.shape[1])


def finish_part(gate, up_proj, d_hidden, gate_weight, up_weight):
    sources, count, hidden_units = gate.shape
    gate = gate.reshape(sources * count, hidden_units)
    up_proj = up_proj.reshape(sources * count, hidden_units)
    d_hidden = d_hidden.reshape(sources * count, hidden_units)
    sigmoid_gate = jax.nn.sigmoid(gate)
    activated = gate * sigmoid_gate
    hidden = activated * up_proj
    gate_grad = jnp.sum(d_hidden * hidden, axis=-1).astype(jnp.bfloat16)
    d_up = (d_hidden * activated).astype(jnp.bfloat16)
    d_gate = (d_hidden * up_proj * sigmoid_gate * (1.0 + gate * (1.0 - sigmoid_gate))).astype(
        jnp.bfloat16
    )
    contract_last = (((1,), (1,)), ((), ()))
    route_grad = lax.dot_general(
        d_gate, gate_weight, contract_last, preferred_element_type=jnp.float32
    )
    route_grad = route_grad + lax.dot_general(
        d_up, up_weight, contract_last, preferred_element_type=jnp.float32
    )
    width = route_grad.shape[1]
    return (
        route_grad.astype(jnp.bfloat16).reshape(sources, count, width),
        gate_grad.reshape(sources, count),
    )


def local(tokens, out_grad, gates, expert_ids, w_gate, w_up, w_down):
    local_tokens = tokens[0]
    local_grads = out_grad[0]
    gate_values = gates[0]
    routes = expert_ids[0]
    gate_weight = w_gate[0, 0]
    up_weight = w_up[0, 0]
    down_weight = w_down[0, 0]
    tok_rows, top_count = routes.shape
    width = local_tokens.shape[1]
    groups = lax.axis_size("expert")
    experts = groups * w_gate.shape[1]
    capacity = max(2, 2 * tok_rows * top_count // experts)
    flat_routes = routes.reshape(-1)
    one_hot = (flat_routes[:, None] == jnp.arange(experts, dtype=jnp.int32)[None, :]).astype(
        jnp.int32
    )
    route_rank = jnp.cumsum(one_hot, axis=0) - one_hot
    slot_index = jnp.sum(route_rank * one_hot, axis=1)
    position = (flat_routes * capacity + slot_index).reshape(tok_rows, top_count)
    placement = (
        position[None, :, :] == jnp.arange(experts * capacity, dtype=jnp.int32)[:, None, None]
    )
    placement = jnp.any(placement, axis=-1).astype(jnp.bfloat16)
    send_tokens = jnp.dot(placement, local_tokens, preferred_element_type=jnp.float32).astype(
        jnp.bfloat16
    )
    send_grads = jnp.dot(placement, local_grads, preferred_element_type=jnp.float32).astype(
        jnp.bfloat16
    )
    send_tokens = send_tokens.reshape(experts, capacity, width)
    send_grads = send_grads.reshape(experts, capacity, width)
    gate, up_proj = forward_part(
        lax.all_to_all(send_tokens, "expert", split_axis=0, concat_axis=0, tiled=True),
        gate_weight,
        up_weight,
    )
    d_hidden = down_part(
        lax.all_to_all(send_grads, "expert", split_axis=0, concat_axis=0, tiled=True), down_weight
    )
    route_grad, gate_grad = finish_part(gate, up_proj, d_hidden, gate_weight, up_weight)
    back_rows = lax.all_to_all(route_grad, "expert", split_axis=0, concat_axis=0, tiled=True)
    back_gates = lax.all_to_all(gate_grad, "expert", split_axis=0, concat_axis=0, tiled=True)
    flat_rows = back_rows.reshape(experts * capacity, width)
    picked = flat_rows[position]
    section_grad = jnp.sum(picked.astype(jnp.float32) * gate_values[:, :, None], axis=1).astype(
        jnp.bfloat16
    )
    grad_gates = back_gates.reshape(-1)[position]
    arrived = passed_along(section_grad, "pipe", -1)
    return (arrived[None], grad_gates[None])


def solution(mesh):
    in_specs = (
        P("pipe", "expert", None),
        P("pipe", "expert", None),
        P("pipe", "expert", None),
        P("pipe", "expert", None),
        P("pipe", "expert", None, None),
        P("pipe", "expert", None, None),
        P("pipe", "expert", None, None),
    )
    out_specs = (P("pipe", "expert", None), P("pipe", "expert", None))
    return jax.shard_map(local, mesh=mesh, in_specs=in_specs, out_specs=out_specs, check_vma=False)
```

profile of v0, /device:TPU:0, one launch (start us, length us, event | category | flops | bytes accessed | tf_op | source)
XLA Modules:
  0.0 207.5 jit_solution(14810109011799801366)
XLA Ops:
  0.6 0.0 copy-start
  0.6 0.9 copy.22
  1.6 0.1 eq.44
  1.7 0.1 eq.40
  1.9 0.6 reduce-window.6
  2.5 0.2 slice_reduce_fusion
  2.7 0.1 fusion.19
  2.8 0.1 reduce_sum.32
  3.0 0.1 copy.25
  3.0 0.1 fusion.16
  3.1 3.1 %convolution_convert_fusion = bf16[512,2048]{1,0:T(8,128)(2,1)} fusion(pred[512,128]{1,0:T(8,128)(4,1)S(1)} %fusion.16, bf16[1,128,2048]{2,1,0:T(8,128)(2,1)} %param.7), kind=kOutput, calls=%fused_computation.13 | convolution fusion | flops 269484032 | bytes 2686976 | tf_op jit(solution)/shard_map/dot_general | solution.py:86
  6.2 7.2 %all-to-all-start.1 = ((bf16[8,64,2048]{2,1,0:T(8,128)(2,1)}), bf16[8,64,2048]{2,1,0:T(8,128)(2,1)}, u32[]{:S(2)}, u32[]{:S(2)}) async-start(bf16[8,64,2048]{2,1,0:T(8,128)(2,1)} %bitcast.53), calls=%async_computation.1 | async-start | bytes 4194304 | tf_op jit(solution)/shard_map/all_to_all | solution.py:95
  13.4 3.0 %convolution_convert_fusion.1 = bf16[512,2048]{1,0:T(8,128)(2,1)} fusion(pred[512,128]{1,0:T(8,128)(4,1)S(1)} %fusion.16, bf16[1,128,2048]{2,1,0:T(8,128)(2,1)} %param.8), kind=kOutput, calls=%fused_computation.14 | convolution fusion | flops 269484032 | bytes 2686976 | tf_op jit(solution)/shard_map/dot_general | solution.py:89
  16.5 45.3 %all-to-all-done.1 = bf16[8,64,2048]{2,1,0:T(8,128)(2,1)} async-done(((bf16[8,64,2048]{2,1,0:T(8,128)(2,1)}), bf16[8,64,2048]{2,1,0:T(8,128)(2,1)}, u32[]{:S(2)}, u32[]{:S(2)}) %all-to-all-start.1) | async-done | bytes 2097184 | tf_op jit(solution)/shard_map/all_to_all | solution.py:95
  61.8 4.3 %all-to-all-start = ((bf16[8,64,2048]{2,1,0:T(8,128)(2,1)}), bf16[8,64,2048]{2,1,0:T(8,128)(2,1)}, u32[]{:S(2)}, u32[]{:S(2)}) async-start(bf16[8,64,2048]{2,1,0:T(8,128)(2,1)} %bitcast.52), calls=%async_computation | async-start | bytes 4194304 | tf_op jit(solution)/shard_map/all_to_all | solution.py:100
  66.1 0.0 copy-done
  66.1 0.0 copy-start.2
  66.2 4.7 %fusion.2 = f32[512,768]{1,0:T(8,128)} fusion(bf16[512,2048]{1,0:T(8,128)(2,1)} %bitcast.9, bf16[1,1,2048,768]{3,2,1,0:T(8,128)(2,1)S(1)} %copy-done), kind=kOutput, calls=%fused_computation.5 | convolution fusion | flops 1610612736 | bytes 6815744 | tf_op jit(solution)/shard_map/dot_general | solution.py:16
  70.8 0.0 copy-done.2
  70.8 4.6 %fusion.6 = f32[512,768]{1,0:T(8,128)} fusion(bf16[512,2048]{1,0:T(8,128)(2,1)} %bitcast.9, bf16[1,1,2048,768]{3,2,1,0:T(8,128)(2,1)S(1)} %copy-done.2), kind=kOutput, calls=%fused_computation.9 | convolution fusion | flops 1610612736 | bytes 6815744 | tf_op jit(solution)/shard_map/dot_general | solution.py:17
  75.5 38.5 %all-to-all-done = bf16[8,64,2048]{2,1,0:T(8,128)(2,1)} async-done(((bf16[8,64,2048]{2,1,0:T(8,128)(2,1)}), bf16[8,64,2048]{2,1,0:T(8,128)(2,1)}, u32[]{:S(2)}, u32[]{:S(2)}) %all-to-all-start) | async-done | bytes 2097184 | tf_op jit(solution)/shard_map/all_to_all | solution.py:100
  114.0 0.0 copy-start.4
  114.0 0.0 copy-start.5
  114.0 5.6 %multiply_reduce_fusion.1 = (bf16[512]{0:T(512)(128)(2,1)S(1)}, f32[512,768]{1,0:T(8,128)S(1)}) fusion(f32[512,768]{1,0:T(8,128)} %fusion.6, f32[512,768]{1,0:T(8,128)} %fusion.2, bf16[512,2048]{1,0:T(8,128)(2,1)} %bitcast.5, bf16[1,1,768,2048]{3,2,1,0:T(8,128)(2,1)} %param.13), kind=kOutput, calls=%fused_computation.16 | convolution fusion | flops 1613364736 | bytes 9962496 | tf_op jit(solution)/shard_map/dot_general | solution.py:29
  119.6 0.0 copy-done.4
  119.6 0.0 copy-done.5
  119.6 0.0 copy-start.3
  119.6 2.3 %fusion = f32[512,2048]{1,0:T(8,128)S(1)} fusion(bf16[1,1,2048,768]{3,2,1,0:T(8,128)(2,1)S(1)} %copy-done, f32[512,768]{1,0:T(8,128)S(1)} %copy-done.4, f32[512,768]{1,0:T(8,128)S(1)} %get-tuple-element.9, f32[512,768]{1,0:T(8,128)S(1)} %copy-done.5), kind=kOutput, calls=%fused_computation.3 | convolution fusion | flops 1614544896 | bytes 12058624 | tf_op jit(solution)/shard_map/dot_general | solution.py:49
  121.9 0.0 copy-done.3
  121.9 3.2 %add_convert_fusion = bf16[512,2048]{1,0:T(8,128)(2,1)} fusion(f32[512,2048]{1,0:T(8,128)S(1)} %fusion, bf16[1,1,2048,768]{3,2,1,0:T(8,128)(2,1)S(1)} %copy-done.3, f32[512,768]{1,0:T(8,128)S(1)} %get-tuple-element.9, f32[512,768]{1,0:T(8,128)S(1)} %copy-done.4), kind=kOutput, calls=%fused_computation.2 | convolution fusion | flops 1615069184 | bytes 12582912 | tf_op jit(solution)/shard_map/dot_general | solution.py:52
  125.1 4.7 %all-to-all-start.2 = ((bf16[8,64,2048]{2,1,0:T(8,128)(2,1)}), bf16[8,64,2048]{2,1,0:T(8,128)(2,1)}, u32[]{:S(2)}, u32[]{:S(2)}) async-start(bf16[8,64,2048]{2,1,0:T(8,128)(2,1)} %bitcast.54), calls=%async_computation.2 | async-start | bytes 4194304 | tf_op jit(solution)/shard_map/all_to_all | solution.py:103
  129.7 0.1 reduce_sum.33
  129.9 0.1 reshape.104
  130.0 0.0 copy-done.1
  130.0 0.1 copy.26
  130.2 47.3 %all-to-all-done.2 = bf16[8,64,2048]{2,1,0:T(8,128)(2,1)} async-done(((bf16[8,64,2048]{2,1,0:T(8,128)(2,1)}), bf16[8,64,2048]{2,1,0:T(8,128)(2,1)}, u32[]{:S(2)}, u32[]{:S(2)}) %all-to-all-start.2) | async-done | bytes 2097184 | tf_op jit(solution)/shard_map/all_to_all | solution.py:103
  177.5 5.2 %gather_fusion = bf16[256,2048]{1,0:T(8,128)(2,1)} fusion(bf16[512,2048]{1,0:T(8,128)(2,1)} %bitcast.13, s32[1024]{0:T(1024)S(1)} %pad_clamp_fusion), kind=kCustom, calls=%fused_computation | custom fusion | bytes 2098176 | tf_op jit(solution)/shard_map/gather | solution.py:106
  182.7 3.4 %reshape.121 = f32[128,2,2048]{2,1,0:T(2,128)} reshape(bf16[256,2048]{1,0:T(8,128)(2,1)} %gather_fusion) | data formatting | bytes 3145728 | tf_op jit(solution)/shard_map/convert_element_type | solution.py:107
  186.1 5.6 %multiply_reduce_fusion = bf16[128,2048]{1,0:T(8,128)(2,1)} fusion(f32[128,2,2048]{2,1,0:T(2,128)} %reshape.121, f32[128,2]{1,0:T(8,128)S(1)} %copy.26), kind=kLoop, calls=%fused_computation.15 | loop fusion | flops 786432 | bytes 2622464 | tf_op jit(solution)/shard_map/reduce_sum | solution.py:107
  191.7 1.3 collective-permute-start
  193.0 0.1 convert_element_type.55
  193.0 9.8 %all_to_all.21 = bf16[8,1,64]{2,1,0:T(2,128)(2,1)S(1)} all-to-all(bf16[8,1,64]{2,1,0:T(2,128)(2,1)S(1)} %convert_element_type.55), channel_id=1, replica_groups=mesh['pipe'=4,'expert'=8] {'expert'}, dimensions={0} | all-to-all | bytes 2048 | tf_op jit(solution)/shard_map/all_to_all | solution.py:104
  202.8 0.1 reshape.101
  202.9 1.9 gather_fusion.1
  204.9 0.2 broadcast_in_dim.5
  205.0 0.6 copy.28
  205.6 0.0 collective-permute-done
  205.6 1.9 copy.30
  (8 shorter events, 0.1 us)
Async XLA Ops:
  0.6 65.5 %copy-start = (bf16[1,1,2048,768]{3,2,1,0:T(8,128)(2,1)S(1)}, bf16[1,1,2048,768]{3,2,1,0:T(8,128)(2,1)}, u32[]{:S(2)}) copy-start(bf16[1,1,2048,768]{3,2,1,0:T(8,128)(2,1)} %param.11) | copy-start | bytes 9437188
  6.2 55.6 %all-to-all-start.1 = ((bf16[8,64,2048]{2,1,0:T(8,128)(2,1)}), bf16[8,64,2048]{2,1,0:T(8,128)(2,1)}, u32[]{:S(2)}, u32[]{:S(2)}) async-start(bf16[8,64,2048]{2,1,0:T(8,128)(2,1)} %bitcast.53), calls=%async_computation.1 | async-start | bytes 4194304 | tf_op jit(solution)/shard_map/all_to_all | solution.py:95
  61.8 52.2 %all-to-all-start = ((bf16[8,64,2048]{2,1,0:T(8,128)(2,1)}), bf16[8,64,2048]{2,1,0:T(8,128)(2,1)}, u32[]{:S(2)}, u32[]{:S(2)}) async-start(bf16[8,64,2048]{2,1,0:T(8,128)(2,1)} %bitcast.52), calls=%async_computation | async-start | bytes 4194304 | tf_op jit(solution)/shard_map/all_to_all | solution.py:100
  66.1 4.7 %copy-start.2 = (bf16[1,1,2048,768]{3,2,1,0:T(8,128)(2,1)S(1)}, bf16[1,1,2048,768]{3,2,1,0:T(8,128)(2,1)}, u32[]{:S(2)}) copy-start(bf16[1,1,2048,768]{3,2,1,0:T(8,128)(2,1)} %param.12) | copy-start | bytes 9437188
  114.0 5.6 %copy-start.4 = (f32[512,768]{1,0:T(8,128)S(1)}, f32[512,768]{1,0:T(8,128)}, u32[]{:S(2)}) copy-start(f32[512,768]{1,0:T(8,128)} %fusion.2) | copy-start | bytes 4718596
  114.0 5.6 %copy-start.5 = (f32[512,768]{1,0:T(8,128)S(1)}, f32[512,768]{1,0:T(8,128)}, u32[]{:S(2)}) copy-start(f32[512,768]{1,0:T(8,128)} %fusion.6) | copy-start | bytes 4718596
  119.6 2.3 %copy-start.3 = (bf16[1,1,2048,768]{3,2,1,0:T(8,128)(2,1)S(1)}, bf16[1,1,2048,768]{3,2,1,0:T(8,128)(2,1)}, u32[]{:S(2)}) copy-start(bf16[1,1,2048,768]{3,2,1,0:T(8,128)(2,1)} %param.12) | copy-start | bytes 9437188
  125.1 5.0 %copy-start.1 = (f32[1,128,2]{1,2,0:T(2,128)S(1)}, f32[1,128,2]{1,2,0:T(2,128)}, u32[]{:S(2)}) copy-start(f32[1,128,2]{1,2,0:T(2,128)} %param.9) | copy-start | bytes 3076
  125.1 52.4 %all-to-all-start.2 = ((bf16[8,64,2048]{2,1,0:T(8,128)(2,1)}), bf16[8,64,2048]{2,1,0:T(8,128)(2,1)}, u32[]{:S(2)}, u32[]{:S(2)}) async-start(bf16[8,64,2048]{2,1,0:T(8,128)(2,1)} %bitcast.54), calls=%async_computation.2 | async-start | bytes 4194304 | tf_op jit(solution)/shard_map/all_to_all | solution.py:103
  191.7 14.0 %collective-permute-start = (bf16[128,2048]{1,0:T(8,128)(2,1)}, bf16[128,2048]{1,0:T(8,128)(2,1)}, u32[]{:S(2)}, u32[]{:S(2)}) collective-permute-start(bf16[128,2048]{1,0:T(8,128)(2,1)} %multiply_reduce_fusion), channel_id=1, source_target_pairs={{8,0},{16,8},{24,16},{9,1},{17,9},{25,17},{10,2},{18,10},{26,18},{... | collective-permute-start | bytes 1572872 | tf_op jit(solution)/shard_map/ppermute | solution.py:10
where the time goes:
time: 208 us
  waiting for transfers between devices  131 us (63%)
  matrix products  26.5 us (13%)
  starting transfers between devices  17.5 us (8%)
  local copies, waits for them, and re-layouts  15.4 us (7%)
  blocking collectives  9.78 us (5%)
  other arithmetic  6.44 us (3%)
    all_to_all x1, waiting for transfers between devices, local(): lax.all_to_all(route_grad, 'expert', split_axis=0, concat_axis=0, tiled=T...  47.3 us
    all_to_all x1, waiting for transfers between devices, local(): lax.all_to_all(send_tokens, 'expert', split_axis=0, concat_axis=0, tiled=...  45.3 us
    all_to_all x1, waiting for transfers between devices, local(): lax.all_to_all(send_grads, 'expert', split_axis=0, concat_axis=0, tiled=T...  38.5 us
    all_to_all x1, blocking collectives, local(): lax.all_to_all(gate_grad, 'expert', split_axis=0, concat_axis=0, tiled=True)  9.78 us
    all_to_all x1, starting transfers between devices, local(): lax.all_to_all(send_tokens, 'expert', split_axis=0, concat_axis=0, tiled=...  7.25 us
    dot_general x1, matrix products, down_part(): lax.dot_general(row_grads, down_weight, contract_last, preferred_element_...  5.62 us
    reduce_sum x1, other arithmetic, local(): jnp.sum(picked.astype(jnp.float32) * gate_values[:, :, None], axis=1)  5.59 us
    gather x1, local copies, waits for them, and re-layouts, local(): picked = flat_rows[position]  5.21 us
  transfers between devices with their start and end apart: 4, of which 3 were waited for; matrix products, arithmetic and copies ran while one was open for 8% of the time, Pallas kernels for 0%

commit v1 on v0

v1 whole, which is shorter than its diff:
```python
import functools
import jax
import jax.numpy as jnp
from jax import lax
from jax.experimental import pallas as pl
from jax.experimental.pallas import tpu as pltpu
from jax.sharding import PartitionSpec as P

F32 = jnp.float32
BF16 = jnp.bfloat16
CHUNKS = 4


def kernel(
    pipes, zs, xs, cap,
    tok_ref, grad_ref, ids_ref, gates_ref, wg_ref, wu_ref, wd_ref,
    out_ref, gg_ref,
    wg, wu, wd, blk, sel_out, sel_in, gate_s, up_s, dh_s, dgate_s, dup_s, slot_gate,
    ret_out, ret_in, part, chain, stage, meta, ggbuf, ggout,
    w_sem, own_sem, own_send, fwd_send, blk_recv, xs_send, xs_recv, m_send, m_recv,
    g_send, g_recv, xr_send, xr_recv, ch_send, ch_recv, p_send, p_recv,
):
    n = zs * xs
    pipe = lax.axis_index("pipe")
    me = lax.axis_index("expert")
    z, x = me // xs, me % xs
    rows, width = tok_ref.shape
    cols = width // CHUNKS
    slots = xs * cap
    hidden = wg.shape[1]
    htile = 256
    mesh_ids = pl.DeviceIdType.MESH

    def remote(src, dst, ssem, rsem, **dev):
        return pltpu.make_async_remote_copy(
            src_ref=src, dst_ref=dst, send_sem=ssem, recv_sem=rsem,
            device_id=dev, device_id_type=mesh_ids,
        )

    loads = [
        pltpu.make_async_copy(wg_ref, wg, w_sem.at[0]),
        pltpu.make_async_copy(wu_ref, wu, w_sem.at[1]),
        pltpu.make_async_copy(wd_ref, wd, w_sem.at[2]),
    ]
    owns = [
        pltpu.make_async_copy(tok_ref, blk.at[0, z], own_sem.at[0]),
        pltpu.make_async_copy(grad_ref, blk.at[1, z], own_sem.at[1]),
    ]
    for c in owns + loads:
        c.start()

    barrier = pltpu.get_barrier_semaphore()
    prev_pipe = lax.rem(pipe + pipes - 1, pipes)
    next_pipe = lax.rem(pipe + 1, pipes)
    for i in range(1, n):
        pl.semaphore_signal(
            barrier, inc=1, device_id={"expert": lax.rem(me + i, n)}, device_id_type=mesh_ids
        )
    for other in (prev_pipe, next_pipe):
        pl.semaphore_signal(barrier, inc=1, device_id={"pipe": other}, device_id_type=mesh_ids)
    pl.semaphore_wait(barrier, n + 1)

    def own_copy(k, up):
        src = (tok_ref, grad_ref)[k]
        return remote(
            src, blk.at[k, z], own_send.at[up, k], blk_recv.at[k, z],
            expert=me + xs if up else me - xs,
        )

    for k in range(2):
        @pl.when(z < zs - 1)
        def _():
            own_copy(k, 1).start()

        @pl.when(z > 0)
        def _():
            own_copy(k, 0).start()

    ids = ids_ref[...]
    sub = lax.broadcasted_iota(jnp.int32, (n, rows), 0)
    hot0 = (sub == ids[0:1]).astype(F32)
    hot1 = (sub == ids[1:2]).astype(F32)
    before = (
        lax.broadcasted_iota(jnp.int32, (rows, rows), 0)
        < lax.broadcasted_iota(jnp.int32, (rows, rows), 1)
    ).astype(F32).astype(BF16)
    earlier = jnp.dot((hot0 + hot1).astype(BF16), before, preferred_element_type=F32)
    idf = ids.astype(F32) * cap
    pos0 = idf[0:1] + jnp.sum(hot0 * earlier, axis=0, keepdims=True)
    pos1 = idf[1:2] + jnp.sum(hot1 * earlier, axis=0, keepdims=True)
    meta[me, 0:1] = pos0
    meta[me, 1:2] = pos1
    meta[me, 2:4] = gates_ref[...]
    meta[me, 4:8] = jnp.zeros((4, rows), F32)

    def meta_copy(i):
        return remote(
            meta.at[me], meta.at[me], m_send.at[i], m_recv.at[me], expert=lax.rem(me + i, n)
        )

    def meta_wait(i):
        e = lax.rem(me + i, n)
        remote(meta.at[e], meta.at[e], m_send.at[i], m_recv.at[e], expert=e).wait_recv()

    for i in range(1, n):
        meta_copy(i).start()
    for i in range(1, n):
        meta_wait(i)

    def onehot(e, first, count):
        want = (first + lax.broadcasted_iota(jnp.int32, (count, rows), 0)).astype(F32)
        m = meta[e]
        return (want == m[0:1]).astype(F32), (want == m[1:2]).astype(F32), m

    def fwd_copy(k, zp):
        return remote(
            blk.at[k, zp], blk.at[k, zp], fwd_send.at[k, zp], blk_recv.at[k, zp],
            expert=jnp.where(zp > z, me - xs, me + xs),
        )

    def can_fwd(zp):
        return ((zp > z) & (z > 0)) | ((zp < z) & (z < zs - 1))

    def xsel_copy(k, zp, i):
        to = lax.rem(x + i, xs)
        return remote(
            sel_out.at[k, zp, to], sel_in.at[k, zp, x], xs_send.at[k, zp, i],
            xs_recv.at[k, zp, x], expert=z * xs + to,
        )

    def xsel_wait(k, zp, i):
        fr = lax.rem(x + i, xs)
        remote(
            sel_out.at[k, zp, fr], sel_in.at[k, zp, fr], xs_send.at[k, zp, i],
            xs_recv.at[k, zp, fr], expert=z * xs + fr,
        ).wait_recv()

    def xret_copy(zp, c, i):
        to = lax.rem(x + i, xs)
        return remote(
            ret_out.at[zp, c, to], ret_in.at[zp, c, x], xr_send.at[zp, c, i],
            xr_recv.at[zp, c, x], expert=z * xs + to,
        )

    def xret_wait(zp, c, i):
        fr = lax.rem(x + i, xs)
        remote(
            ret_out.at[zp, c, fr], ret_in.at[zp, c, fr], xr_send.at[zp, c, i],
            xr_recv.at[zp, c, fr], expert=z * xs + fr,
        ).wait_recv()

    def chain_copy(zp, c):
        up = (zp > z).astype(jnp.int32)
        return remote(
            part.at[zp, c], chain.at[up, zp, c], ch_send.at[zp, c], ch_recv.at[up, zp, c],
            expert=jnp.where(zp > z, me + xs, me - xs),
        )

    def chain_wait(up, zp, c):
        remote(
            part.at[zp, c], chain.at[up, zp, c], ch_send.at[zp, c], ch_recv.at[up, zp, c],
            expert=jnp.where(up == 1, me - xs, me + xs),
        ).wait_recv()

    def gg_copy(e):
        return remote(ggout.at[e], ggbuf.at[me], g_send.at[e], g_recv.at[me], expert=e)

    def gg_wait(e):
        remote(ggout.at[e], ggbuf.at[e], g_send.at[e], g_recv.at[e], expert=e).wait_recv()

    def take(k, zp, d):
        @pl.when(d > 0)
        def _():
            fwd_copy(k, zp).wait_recv()

            @pl.when(can_fwd(zp))
            def _():
                fwd_copy(k, zp).start()

        o0, o1, _ = onehot(zp * xs + x, z * slots, slots)
        hot = (o0 + o1).astype(BF16)

        def col(c, _):
            at = pl.ds(pl.multiple_of(c * cols, cols), cols)
            got = jnp.dot(hot, blk[k, zp, :, at], preferred_element_type=F32).astype(BF16)
            sel_out[k, zp, :, :, at] = got.reshape(xs, cap, cols)
            return 0

        lax.fori_loop(0, CHUNKS, col, 0)
        for i in range(1, xs):
            xsel_copy(k, zp, i).start()
        sel_in[k, zp, x] = sel_out[k, zp, x]

    def work(zp):
        for k in range(2):
            for i in range(1, xs):
                xsel_wait(k, zp, i)
        contract_last = (((1,), (1,)), ((), ()))

        def tile(h, _):
            at = pl.ds(pl.multiple_of(h * htile, htile), htile)
            a = sel_in[0, zp].reshape(slots, width)
            b = sel_in[1, zp].reshape(slots, width)
            gate = jnp.dot(a, wg[:, at], preferred_element_type=F32)
            up = jnp.dot(a, wu[:, at], preferred_element_type=F32)
            dh = lax.dot_general(b, wd[at, :], contract_last, preferred_element_type=F32)
            sig = jax.nn.sigmoid(gate)
            act = gate * sig
            dup_s[:, at] = (dh * act).astype(BF16)
            dgate_s[:, at] = (dh * up * sig * (1.0 + gate * (1.0 - sig))).astype(BF16)
            return _ + jnp.sum(dh * (act * up), axis=-1, keepdims=True)

        gg = lax.fori_loop(0, hidden // htile, tile, jnp.zeros((slots, 1), F32))
        for s in range(xs):
            e = zp * xs + s
            o0, o1, m = onehot(e, me * cap, cap)
            slot_gate[s * cap:(s + 1) * cap] = jnp.sum(
                o0 * m[2:3] + o1 * m[3:4], axis=1, keepdims=True
            )
            mine = gg[s * cap:(s + 1) * cap]
            ggout[e, 0:1] = jnp.sum(o0 * mine, axis=0, keepdims=True)
            ggout[e, 1:2] = jnp.sum(o1 * mine, axis=0, keepdims=True)

            @pl.when(e != me)
            def _():
                gg_copy(e).start()

        def col(c, _):
            at = pl.ds(pl.multiple_of(c * cols, cols), cols)
            r = lax.dot_general(dgate_s[...], wg[at, :], contract_last, preferred_element_type=F32)
            r = r + lax.dot_general(dup_s[...], wu[at, :], contract_last, preferred_element_type=F32)
            r = (r * slot_gate[...]).astype(BF16)
            ret_out[zp, c] = r.reshape(xs, cap, cols)
            for i in range(1, xs):
                xret_copy(zp, c, i).start()
            ret_in[zp, c, x] = ret_out[zp, c, x]
            return 0

        lax.fori_loop(0, CHUNKS, col, 0)

    def combine(zp):
        o0, o1, _ = onehot(zp * xs + x, z * slots, slots)
        hot = (o0 + o1).astype(BF16)
        head = ((z == 0) & (zp > 0)) | ((z == zs - 1) & (zp < z))

        def col(c, _):
            for i in range(1, xs):
                xret_wait(zp, c, i)
            r = ret_in[zp, c].reshape(slots, cols)
            part[zp, c] = lax.dot_general(
                hot, r, (((0,), (0,)), ((), ())), preferred_element_type=F32
            ).astype(BF16)

            @pl.when(head)
            def _():
                chain_copy(zp, c).start()

            return 0

        lax.fori_loop(0, CHUNKS, col, 0)

    def place(d, side):
        zp = z + d * (1 - 2 * side)
        ok = (zp >= 0) & (zp < zs) & ((d > 0) | (side == 0))
        return zp, ok

    def sides(d, fn):
        def one(side, _):
            zp, ok = place(d, side)

            @pl.when(ok)
            def _():
                fn(zp)

            return 0

        lax.fori_loop(0, 2, one, 0)

    for c in owns:
        c.wait()
    for c in loads:
        c.wait()

    def step(d, _):
        for k in range(2):
            sides(d, lambda zp: take(k, zp, d))
        sides(d, work)
        sides(d, combine)
        return 0

    lax.fori_loop(0, zs, step, 0)

    def relay(up, zp):
        def col(c, _):
            chain_wait(up, zp, c)
            part[zp, c] = (part[zp, c].astype(F32) + chain[up, zp, c].astype(F32)).astype(BF16)
            chain_copy(zp, c).start()
            return 0

        lax.fori_loop(0, CHUNKS, col, 0)

    def hop(k, _):
        down = zs - 1 - k

        @pl.when((z > 0) & (z < k))
        def _():
            relay(1, k)

        @pl.when((z < zs - 1) & (z > down))
        def _():
            relay(0, down)

        return 0

    lax.fori_loop(1, zs, hop, 0)

    def pipe_copy(c):
        at = pl.ds(c * cols, cols)
        return remote(
            stage.at[c], out_ref.at[:, at], p_send.at[c], p_recv.at[c], pipe=prev_pipe
        )

    for c in range(CHUNKS):
        stage[c] = part[z, c]
        has_below, has_above = z > 0, z < zs - 1

        @pl.when(has_below & has_above)
        def _():
            chain_wait(1, z, c)
            chain_wait(0, z, c)
            stage[c] = (
                part[z, c].astype(F32) + chain[1, z, c].astype(F32) + chain[0, z, c].astype(F32)
            ).astype(BF16)

        @pl.when(has_below & (z == zs - 1))
        def _():
            chain_wait(1, z, c)
            stage[c] = (part[z, c].astype(F32) + chain[1, z, c].astype(F32)).astype(BF16)

        @pl.when(has_above & (z == 0))
        def _():
            chain_wait(0, z, c)
            stage[c] = (part[z, c].astype(F32) + chain[0, z, c].astype(F32)).astype(BF16)

        @pl.when(pipe > 0)
        def _():
            pipe_copy(c).start()

    for i in range(1, n):
        gg_wait(lax.rem(me + i, n))
    ggbuf[me] = ggout[me]
    total = ggbuf[0]
    for e in range(1, n):
        total = total + ggbuf[e]
    gg_ref[...] = total.astype(BF16)

    for k in range(2):
        @pl.when(z < zs - 1)
        def _():
            own_copy(k, 1).wait_send()

        @pl.when(z > 0)
        def _():
            own_copy(k, 0).wait_send()

    def drain(zp, _):
        @pl.when(can_fwd(zp))
        def _():
            for k in range(2):
                fwd_copy(k, zp).wait_send()

        for i in range(1, xs):
            for k in range(2):
                xsel_copy(k, zp, i).wait_send()

            def xcol(c, _):
                xret_copy(zp, c, i).wait_send()
                return 0

            lax.fori_loop(0, CHUNKS, xcol, 0)

        @pl.when(zp != z)
        def _():
            def ccol(c, _):
                chain_copy(zp, c).wait_send()
                return 0

            lax.fori_loop(0, CHUNKS, ccol, 0)

        return 0

    lax.fori_loop(0, zs, drain, 0)
    for i in range(1, n):
        meta_copy(i).wait_send()
        gg_copy(lax.rem(me + i, n)).wait_send()

    @pl.when(pipe > 0)
    def _():
        for c in range(CHUNKS):
            pipe_copy(c).wait_send()

    @pl.when(pipe < pipes - 1)
    def _():
        for c in range(CHUNKS):
            pipe_copy(c).wait_recv()

    @pl.when(pipe == pipes - 1)
    def _():
        out_ref[...] = jnp.zeros(out_ref.shape, BF16)


def local(pipes, tokens, out_grad, gates, expert_ids, w_gate, w_up, w_down):
    rows, width = tokens.shape[1:]
    top = expert_ids.shape[2]
    n = lax.axis_size("expert")
    xs = 1 << ((n.bit_length() - 1) // 2)
    zs = n // xs
    cap = max(2, 2 * rows * top // n)
    hidden = w_gate.shape[3]
    slots = xs * cap
    cols = width // CHUNKS
    dma = pltpu.SemaphoreType.DMA
    vmem = pl.BlockSpec(memory_space=pltpu.VMEM)
    hbm = pl.BlockSpec(memory_space=pl.ANY)
    arrived, gg = pl.pallas_call(
        functools.partial(kernel, pipes, zs, xs, cap),
        out_shape=(
            jax.ShapeDtypeStruct((rows, width), BF16),
            jax.ShapeDtypeStruct((top, rows), BF16),
        ),
        in_specs=[hbm, hbm, vmem, vmem, hbm, hbm, hbm],
        out_specs=(vmem, vmem),
        scratch_shapes=[
            pltpu.VMEM((width, hidden), BF16),
            pltpu.VMEM((width, hidden), BF16),
            pltpu.VMEM((hidden, width), BF16),
            pltpu.VMEM((2, zs, rows, width), BF16),
            pltpu.VMEM((2, zs, xs, cap, width), BF16),
            pltpu.VMEM((2, zs, xs, cap, width), BF16),
            pltpu.VMEM((8, 128), F32),
            pltpu.VMEM((8, 128), F32),
            pltpu.VMEM((8, 128), F32),
            pltpu.VMEM((slots, hidden), BF16),
            pltpu.VMEM((slots, hidden), BF16),
            pltpu.VMEM((slots, 1), F32),
            pltpu.VMEM((zs, CHUNKS, xs, cap, cols), BF16),
            pltpu.VMEM((zs, CHUNKS, xs, cap, cols), BF16),
            pltpu.VMEM((zs, CHUNKS, rows, cols), BF16),
            pltpu.VMEM((2, zs, CHUNKS, rows, cols), BF16),
            pltpu.VMEM((CHUNKS, rows, cols), BF16),
            pltpu.VMEM((n, 8, rows), F32),
            pltpu.VMEM((n, top, rows), F32),
            pltpu.VMEM((n, top, rows), F32),
            dma((3,)),
            dma((2,)),
            dma((2, 2)),
            dma((2, zs)),
            dma((2, zs)),
            dma((2, zs, xs)),
            dma((2, zs, xs)),
            dma((n,)),
            dma((n,)),
            dma((n,)),
            dma((n,)),
            dma((zs, CHUNKS, xs)),
            dma((zs, CHUNKS, xs)),
            dma((zs, CHUNKS)),
            dma((2, zs, CHUNKS)),
            dma((CHUNKS,)),
            dma((CHUNKS,)),
        ],
        compiler_params=pltpu.CompilerParams(
            collective_id=0, has_side_effects=True, vmem_limit_bytes=56 * 1024 * 1024
        ),
    )(
        tokens[0], out_grad[0], expert_ids[0].T, gates[0].T,
        w_gate[0, 0], w_up[0, 0], w_down[0, 0],
    )
    return arrived[None], gg.T[None]


def solution(mesh):
    row = P("pipe", "expert", None)
    weight = P("pipe", "expert", None, None)
    return jax.shard_map(
        functools.partial(local, mesh.shape["pipe"]),
        mesh=mesh,
        in_specs=(row, row, row, row, weight, weight, weight),
        out_specs=(row, row),
        check_vma=False,
    )
```

time: 208 us -> 159 us (0.76)
  Pallas kernels: 0 us -> 155 us
  waiting for transfers between devices: 131 us -> 0 us
  matrix products: 26.5 us -> 0 us
  starting transfers between devices: 17.5 us -> 0 us
  local copies, waits for them, and re-layouts: 15.4 us -> 2.99 us
  blocking collectives: 9.78 us -> 0 us
  other arithmetic: 6.44 us -> 0 us
    pallas_call x0 -> x1, Pallas kernels: none -> 155 us  [local(): pl.pallas_call(functools.partial(kernel, pipes, zs, xs, cap), out_shape=(...]
    all_to_all x3 -> x0, waiting for transfers between devices: 131 us -> none  [the longest x1 47.3 us: local(): lax.all_to_all(route_grad, 'expert', split_axis=0, concat_axis=0, tiled=T...]
    dot_general x7 -> x0, matrix products: 26.5 us -> none  [the longest x1 5.62 us: down_part(): lax.dot_general(row_grads, down_weight, contract_last, preferred_element_...]
    all_to_all x3 -> x0, starting transfers between devices: 16.2 us -> none  [the longest x1 7.25 us: local(): lax.all_to_all(send_tokens, 'expert', split_axis=0, concat_axis=0, tiled=...]
    all_to_all x1 -> x0, blocking collectives: 9.78 us -> none  [local(): lax.all_to_all(gate_grad, 'expert', split_axis=0, concat_axis=0, tiled=True)]
    gather x2 -> x0, local copies, waits for them, and re-layouts: 7.14 us -> none  [the longest x1 5.21 us: local(): picked = flat_rows[position]]
    reduce_sum x2 -> x0, other arithmetic: 5.68 us -> none  [the longest x1 5.59 us: local(): jnp.sum(picked.astype(jnp.float32) * gate_values[:, :, None], axis=1)]
    convert_element_type x2 -> x0, local copies, waits for them, and re-layouts: 3.48 us -> none  [the longest x1 3.39 us: local(): picked.astype(jnp.float32) * gate_values[:, :, None]]
  transfers between devices with their start and end apart: 4 -> 0, of which waited for: 3 -> 0; matrix products, arithmetic and copies ran while one was open for 8% -> 0% of each run, Pallas kernels for 0% -> 0%
where the time goes in v1:
time: 159 us
  Pallas kernels  155 us (97%)
  local copies, waits for them, and re-layouts  2.99 us (2%)
    pallas_call x1, Pallas kernels, local(): pl.pallas_call(functools.partial(kernel, pipes, zs, xs, cap), out_shape=(...  155 us

profile of v1, /device:TPU:0, one launch (start us, length us, event | category | flops | bytes accessed | tf_op | source)
XLA Modules:
  0.0 158.6 jit_solution(18041477452648383912)
XLA Ops:
  0.6 154.9 %shard_map.86 = (bf16[128,2048]{1,0:T(8,128)(2,1)}, bf16[2,128]{1,0:T(2,128)(2,1)}) custom-call(bf16[128,2048]{1,0:T(8,128)(2,1)} %bitcast.18, bf16[128,2048]{1,0:T(8,128)(2,1)} %bitcast.19, s32[2,128]{1,0:T(2,128)} %bitcast.21, f32[2,128]{1,0:T(2,128)} %bitcast.22, bf16[2048,768]{1,0:T(8,128)(2,1)} %bitcast.15, bf16[2048,768]{1,0:T(8,128)(2,1)} %bitcast.16, ...), custom_call_target="tpu_custom_call" | custom-call | tf_op jit(solution)/shard_map/pallas_call | solution.py:425
  155.6 1.9 %copy.11 = bf16[1,128,2048]{2,1,0:T(8,128)(2,1)} copy(bf16[1,128,2048]{2,1,0:T(8,128)(2,1)} %bitcast.20) | data formatting | bytes 1048576
  157.5 1.1 copy.12

commit v2 on v1

--- a/solution.py
+++ b/solution.py
@@ -9,13 +9,14 @@
 F32 = jnp.float32
 BF16 = jnp.bfloat16
 CHUNKS = 4
+PIECES = 2
 
 
 def kernel(
     pipes, zs, xs, cap,
     tok_ref, grad_ref, ids_ref, gates_ref, wg_ref, wu_ref, wd_ref,
     out_ref, gg_ref,
-    wg, wu, wd, blk, sel_out, sel_in, gate_s, up_s, dh_s, dgate_s, dup_s, slot_gate,
+    wg, wu, wd, blk, sel_out, sel_in, gate_s, up_s, dgate_s, dup_s, slot_gate,
     ret_out, ret_in, part, chain, stage, meta, ggbuf, ggout,
     w_sem, own_sem, own_send, fwd_send, blk_recv, xs_send, xs_recv, m_send, m_recv,
     g_send, g_recv, xr_send, xr_recv, ch_send, ch_recv, p_send, p_recv,
@@ -28,6 +29,7 @@
     cols = width // CHUNKS
     slots = xs * cap
     hidden = wg.shape[1]
+    span = width // PIECES
     htile = 256
     mesh_ids = pl.DeviceIdType.MESH
 
@@ -43,8 +45,11 @@
         pltpu.make_async_copy(wd_ref, wd, w_sem.at[2]),
     ]
     owns = [
-        pltpu.make_async_copy(tok_ref, blk.at[0, z], own_sem.at[0]),
-        pltpu.make_async_copy(grad_ref, blk.at[1, z], own_sem.at[1]),
+        pltpu.make_async_copy(
+            (tok_ref, grad_ref)[k].at[:, pl.ds(p * span, span)], blk.at[k, p, z], own_sem.at[k, p]
+        )
+        for k in range(2)
+        for p in range(PIECES)
     ]
     for c in owns + loads:
         c.start()
@@ -60,21 +65,22 @@
         pl.semaphore_signal(barrier, inc=1, device_id={"pipe": other}, device_id_type=mesh_ids)
     pl.semaphore_wait(barrier, n + 1)
 
-    def own_copy(k, up):
-        src = (tok_ref, grad_ref)[k]
-        return remote(
-            src, blk.at[k, z], own_send.at[up, k], blk_recv.at[k, z],
+    def own_copy(k, p, up):
+        src = (tok_ref, grad_ref)[k].at[:, pl.ds(p * span, span)]
+        return remote(
+            src, blk.at[k, p, z], own_send.at[up, k, p], blk_recv.at[k, p, z],
             expert=me + xs if up else me - xs,
         )
 
-    for k in range(2):
+    pieces = [(k, p) for k in range(2) for p in range(PIECES)]
+    for k, p in pieces:
         @pl.when(z < zs - 1)
         def _():
-            own_copy(k, 1).start()
+            own_copy(k, p, 1).start()
 
         @pl.when(z > 0)
         def _():
-            own_copy(k, 0).start()
+            own_copy(k, p, 0).start()
 
     ids = ids_ref[...]
     sub = lax.broadcasted_iota(jnp.int32, (n, rows), 0)
@@ -104,35 +110,33 @@
 
     for i in range(1, n):
         meta_copy(i).start()
-    for i in range(1, n):
-        meta_wait(i)
 
     def onehot(e, first, count):
         want = (first + lax.broadcasted_iota(jnp.int32, (count, rows), 0)).astype(F32)
         m = meta[e]
         return (want == m[0:1]).astype(F32), (want == m[1:2]).astype(F32), m
 
-    def fwd_copy(k, zp):
-        return remote(
-            blk.at[k, zp], blk.at[k, zp], fwd_send.at[k, zp], blk_recv.at[k, zp],
+    def fwd_copy(k, p, zp):
+        return remote(
+            blk.at[k, p, zp], blk.at[k, p, zp], fwd_send.at[k, p, zp], blk_recv.at[k, p, zp],
             expert=jnp.where(zp > z, me - xs, me + xs),
         )
 
     def can_fwd(zp):
         return ((zp > z) & (z > 0)) | ((zp < z) & (z < zs - 1))
 
-    def xsel_copy(k, zp, i):
+    def xsel_copy(k, p, zp, i):
         to = lax.rem(x + i, xs)
         return remote(
-            sel_out.at[k, zp, to], sel_in.at[k, zp, x], xs_send.at[k, zp, i],
-            xs_recv.at[k, zp, x], expert=z * xs + to,
-        )
-
-    def xsel_wait(k, zp, i):
+            sel_out.at[k, p, zp, to], sel_in.at[k, p, zp, x], xs_send.at[k, p, zp, i],
+            xs_recv.at[k, p, zp, x], expert=z * xs + to,
+        )
+
+    def xsel_wait(k, p, zp, i):
         fr = lax.rem(x + i, xs)
         remote(
-            sel_out.at[k, zp, fr], sel_in.at[k, zp, fr], xs_send.at[k, zp, i],
-            xs_recv.at[k, zp, fr], expert=z * xs + fr,
+            sel_out.at[k, p, zp, fr], sel_in.at[k, p, zp, fr], xs_send.at[k, p, zp, i],
+            xs_recv.at[k, p, zp, fr], expert=z * xs + fr,
         ).wait_recv()
 
     def xret_copy(zp, c, i):
@@ -169,41 +173,63 @@
         remote(ggout.at[e], ggbuf.at[e], g_send.at[e], g_recv.at[e], expert=e).wait_recv()
 
     def take(k, zp, d):
-        @pl.when(d > 0)
-        def _():
-            fwd_copy(k, zp).wait_recv()
-
-            @pl.when(can_fwd(zp))
-            def _():
-                fwd_copy(k, zp).start()
-
         o0, o1, _ = onehot(zp * xs + x, z * slots, slots)
         hot = (o0 + o1).astype(BF16)
 
-        def col(c, _):
-            at = pl.ds(pl.multiple_of(c * cols, cols), cols)
-            got = jnp.dot(hot, blk[k, zp, :, at], preferred_element_type=F32).astype(BF16)
-            sel_out[k, zp, :, :, at] = got.reshape(xs, cap, cols)
+        def piece(p, _):
+            @pl.when(d > 0)
+            def _():
+                fwd_copy(k, p, zp).wait_recv()
+
+                @pl.when(can_fwd(zp))
+                def _():
+                    fwd_copy(k, p, zp).start()
+
+            got = jnp.dot(hot, blk[k, p, zp], preferred_element_type=F32).astype(BF16)
+            sel_out[k, p, zp] = got.reshape(xs, cap, span)
+            for i in range(1, xs):
+                xsel_copy(k, p, zp, i).start()
+            sel_in[k, p, zp, x] = sel_out[k, p, zp, x]
             return 0
 
-        lax.fori_loop(0, CHUNKS, col, 0)
-        for i in range(1, xs):
-            xsel_copy(k, zp, i).start()
-        sel_in[k, zp, x] = sel_out[k, zp, x]
+        lax.fori_loop(0, PIECES, piece, 0)
+
+    def xsel_arrived(k, zp):
+        for p in range(PIECES):
+            for i in range(1, xs):
+                xsel_wait(k, p, zp, i)
 
     def work(zp):
-        for k in range(2):
-            for i in range(1, xs):
-                xsel_wait(k, zp, i)
         contract_last = (((1,), (1,)), ((), ()))
+        xsel_arrived(0, zp)
+
+        def tile_up(h, _):
+            at = pl.ds(pl.multiple_of(h * htile, htile), htile)
+            gate = jnp.zeros((slots, htile), F32)
+            up = jnp.zeros((slots, htile), F32)
+            for p in range(PIECES):
+                a = sel_in[0, p, zp].reshape(slots, span)
+                depth = slice(p * span, (p + 1) * span)
+                gate = gate + jnp.dot(a, wg[depth, at], preferred_element_type=F32)
+                up = up + jnp.dot(a, wu[depth, at], preferred_element_type=F32)
+            gate_s[:, at] = gate
+            up_s[:, at] = up
+            return 0
+
+        lax.fori_loop(0, hidden // htile, tile_up, 0)
+        xsel_arrived(1, zp)
 
         def tile(h, _):
             at = pl.ds(pl.multiple_of(h * htile, htile), htile)
-            a = sel_in[0, zp].reshape(slots, width)
-            b = sel_in[1, zp].reshape(slots, width)
-            gate = jnp.dot(a, wg[:, at], preferred_element_type=F32)
-            up = jnp.dot(a, wu[:, at], preferred_element_type=F32)
-            dh = lax.dot_general(b, wd[at, :], contract_last, preferred_element_type=F32)
+            dh = jnp.zeros((slots, htile), F32)
+            for p in range(PIECES):
+                b = sel_in[1, p, zp].reshape(slots, span)
+                depth = slice(p * span, (p + 1) * span)
+                dh = dh + lax.dot_general(
+                    b, wd[at, depth], contract_last, preferred_element_type=F32
+                )
+            gate = gate_s[:, at]
+            up = up_s[:, at]
             sig = jax.nn.sigmoid(gate)
             act = gate * sig
             dup_s[:, at] = (dh * act).astype(BF16)
@@ -261,7 +287,7 @@
 
     def place(d, side):
         zp = z + d * (1 - 2 * side)
-        ok = (zp >= 0) & (zp < zs) & ((d > 0) | (side == 0))
+        ok = (zp >= 0) & (zp < zs) & ((d > 0) | ((d == 0) & (side == 0)))
         return zp, ok
 
     def sides(d, fn):
@@ -278,17 +304,23 @@
 
     for c in owns:
         c.wait()
-    for c in loads:
-        c.wait()
-
-    def step(d, _):
-        for k in range(2):
-            sides(d, lambda zp: take(k, zp, d))
-        sides(d, work)
-        sides(d, combine)
+
+    def step(u, _):
+        d, k = u // 2, u % 2
+        sides(d, lambda zp: take(k, zp, d))
+
+        @pl.when(u == 1)
+        def _():
+            for c in loads:
+                c.wait()
+            for i in range(1, n):
+                meta_wait(i)
+
+        sides(jnp.where(u == 1, 0, jnp.where((k == 0) & (d >= 2), d - 1, -1)), work)
+        sides(jnp.where(k == 1, d - 1, -1), combine)
         return 0
 
-    lax.fori_loop(0, zs, step, 0)
+    lax.fori_loop(0, 2 * zs + 2, step, 0)
 
     def relay(up, zp):
         def col(c, _):
@@ -354,24 +386,24 @@
         total = total + ggbuf[e]
     gg_ref[...] = total.astype(BF16)
 
-    for k in range(2):
+    for k, p in pieces:
         @pl.when(z < zs - 1)
         def _():
-            own_copy(k, 1).wait_send()
+            own_copy(k, p, 1).wait_send()
 
         @pl.when(z > 0)
         def _():
-            own_copy(k, 0).wait_send()
+            own_copy(k, p, 0).wait_send()
 
     def drain(zp, _):
         @pl.when(can_fwd(zp))
         def _():
-            for k in range(2):
-                fwd_copy(k, zp).wait_send()
+            for k, p in pieces:
+                fwd_copy(k, p, zp).wait_send()
 
         for i in range(1, xs):
-            for k in range(2):
-                xsel_copy(k, zp, i).wait_send()
+            for k, p in pieces:
+                xsel_copy(k, p, zp, i).wait_send()
 
             def xcol(c, _):
                 xret_copy(zp, c, i).wait_send()
@@ -419,6 +451,7 @@
     hidden = w_gate.shape[3]
     slots = xs * cap
     cols = width // CHUNKS
+    span = width // PIECES
     dma = pltpu.SemaphoreType.DMA
     vmem = pl.BlockSpec(memory_space=pltpu.VMEM)
     hbm = pl.BlockSpec(memory_space=pl.ANY)
@@ -434,12 +467,11 @@
             pltpu.VMEM((width, hidden), BF16),
             pltpu.VMEM((width, hidden), BF16),
             pltpu.VMEM((hidden, width), BF16),
-            pltpu.VMEM((2, zs, rows, width), BF16),
-            pltpu.VMEM((2, zs, xs, cap, width), BF16),
-            pltpu.VMEM((2, zs, xs, cap, width), BF16),
-            pltpu.VMEM((8, 128), F32),
-            pltpu.VMEM((8, 128), F32),
-            pltpu.VMEM((8, 128), F32),
+            pltpu.VMEM((2, PIECES, zs, rows, span), BF16),
+            pltpu.VMEM((2, PIECES, zs, xs, cap, span), BF16),
+            pltpu.VMEM((2, PIECES, zs, xs, cap, span), BF16),
+            pltpu.VMEM((slots, hidden), F32),
+            pltpu.VMEM((slots, hidden), F32),
             pltpu.VMEM((slots, hidden), BF16),
             pltpu.VMEM((slots, hidden), BF16),
             pltpu.VMEM((slots, 1), F32),
@@ -452,12 +484,12 @@
             pltpu.VMEM((n, top, rows), F32),
             pltpu.VMEM((n, top, rows), F32),
             dma((3,)),
-            dma((2,)),
-            dma((2, 2)),
-            dma((2, zs)),
-            dma((2, zs)),
-            dma((2, zs, xs)),
-            dma((2, zs, xs)),
+            dma((2, PIECES)),
+            dma((2, 2, PIECES)),
+            dma((2, PIECES, zs)),
+            dma((2, PIECES, zs)),
+            dma((2, PIECES, zs, xs)),
+            dma((2, PIECES, zs, xs)),
             dma((n,)),
             dma((n,)),
             dma((n,)),

time: 159 us -> 146 us (0.918)
  Pallas kernels: 155 us -> 142 us
    pallas_call x1, Pallas kernels: 155 us -> 142 us  [local(): pl.pallas_call(functools.partial(kernel, pipes, zs, xs, cap), out_shape=(...]
where the time goes in v2:
time: 146 us; the launch traced here: 145 us
  Pallas kernels  142 us (97%)
  local copies, waits for them, and re-layouts  2.99 us (2%)
    pallas_call x1, Pallas kernels, local(): pl.pallas_call(functools.partial(kernel, pipes, zs, xs, cap), out_shape=(...  142 us
    unnamed x2, local copies, waits for them, and re-layouts  2.99 us

profile of v2, /device:TPU:0, one launch (start us, length us, event | category | flops | bytes accessed | tf_op | source)
XLA Modules:
  0.0 145.3 jit_solution(7112825724248376228)
XLA Ops:
  0.6 141.7 %shard_map.86 = (bf16[128,2048]{1,0:T(8,128)(2,1)}, bf16[2,128]{1,0:T(2,128)(2,1)}) custom-call(bf16[128,2048]{1,0:T(8,128)(2,1)} %bitcast.18, bf16[128,2048]{1,0:T(8,128)(2,1)} %bitcast.19, s32[2,128]{1,0:T(2,128)} %bitcast.21, f32[2,128]{1,0:T(2,128)} %bitcast.22, bf16[2048,768]{1,0:T(8,128)(2,1)} %bitcast.15, bf16[2048,768]{1,0:T(8,128)(2,1)} %bitcast.16, ...), custom_call_target="tpu_custom_call" | custom-call | tf_op jit(solution)/shard_map/pallas_call | solution.py:458
  142.3 1.9 %copy.11 = bf16[1,128,2048]{2,1,0:T(8,128)(2,1)} copy(bf16[1,128,2048]{2,1,0:T(8,128)(2,1)} %bitcast.20) | data formatting | bytes 1048576
  144.2 1.1 copy.12

commit v3 on v2

--- a/solution.py
+++ b/solution.py
@@ -8,8 +8,8 @@
 
 F32 = jnp.float32
 BF16 = jnp.bfloat16
-CHUNKS = 4
-PIECES = 2
+CHUNKS = 2
+PIECES = 1
 
 
 def kernel(
@@ -322,29 +322,31 @@
 
     lax.fori_loop(0, 2 * zs + 2, step, 0)
 
-    def relay(up, zp):
-        def col(c, _):
-            chain_wait(up, zp, c)
-            part[zp, c] = (part[zp, c].astype(F32) + chain[up, zp, c].astype(F32)).astype(BF16)
-            chain_copy(zp, c).start()
+    def relay(up, zp, c):
+        chain_wait(up, zp, c)
+        part[zp, c] = (part[zp, c].astype(F32) + chain[up, zp, c].astype(F32)).astype(BF16)
+        chain_copy(zp, c).start()
+
+    def hop(i, _):
+        k, c = 1 + i // CHUNKS, i % CHUNKS
+        down = zs - 1 - k
+
+        def turn(t, _):
+            up = jnp.where(z < zs // 2, 1 - t, t)
+
+            @pl.when((up == 1) & (z > 0) & (z < k))
+            def _():
+                relay(1, k, c)
+
+            @pl.when((up == 0) & (z < zs - 1) & (z > down))
+            def _():
+                relay(0, down, c)
+
             return 0
 
-        lax.fori_loop(0, CHUNKS, col, 0)
-
-    def hop(k, _):
-        down = zs - 1 - k
-
-        @pl.when((z > 0) & (z < k))
-        def _():
-            relay(1, k)
-
-        @pl.when((z < zs - 1) & (z > down))
-        def _():
-            relay(0, down)
-
-        return 0
-
-    lax.fori_loop(1, zs, hop, 0)
+        return lax.fori_loop(0, 2, turn, 0)
+
+    lax.fori_loop(0, (zs - 1) * CHUNKS, hop, 0)
 
     def pipe_copy(c):
         at = pl.ds(c * cols, cols)

time: 146 us -> 136 us (0.932)
  Pallas kernels: 142 us -> 131 us
    pallas_call x1, Pallas kernels: 142 us -> 131 us  [local(): pl.pallas_call(functools.partial(kernel, pipes, zs, xs, cap), out_shape=(...]
where the time goes in v3:
time: 136 us; the launch traced here: 135 us
  Pallas kernels  131 us (96%)
  local copies, waits for them, and re-layouts  2.99 us (2%)
    pallas_call x1, Pallas kernels, local(): pl.pallas_call(functools.partial(kernel, pipes, zs, xs, cap), out_shape=(...  131 us
    unnamed x2, local copies, waits for them, and re-layouts  2.99 us

profile of v3, /device:TPU:0, one launch (start us, length us, event | category | flops | bytes accessed | tf_op | source)
XLA Modules:
  0.0 134.9 jit_solution(9143403649996308802)
XLA Ops:
  0.6 131.2 %shard_map.86 = (bf16[128,2048]{1,0:T(8,128)(2,1)}, bf16[2,128]{1,0:T(2,128)(2,1)}) custom-call(bf16[128,2048]{1,0:T(8,128)(2,1)} %bitcast.18, bf16[128,2048]{1,0:T(8,128)(2,1)} %bitcast.19, s32[2,128]{1,0:T(2,128)} %bitcast.21, f32[2,128]{1,0:T(2,128)} %bitcast.22, bf16[2048,768]{1,0:T(8,128)(2,1)} %bitcast.15, bf16[2048,768]{1,0:T(8,128)(2,1)} %bitcast.16, ...), custom_call_target="tpu_custom_call" | custom-call | tf_op jit(solution)/shard_map/pallas_call | solution.py:460
  131.9 1.9 %copy.11 = bf16[1,128,2048]{2,1,0:T(8,128)(2,1)} copy(bf16[1,128,2048]{2,1,0:T(8,128)(2,1)} %bitcast.20) | data formatting | bytes 1048576
  133.7 1.1 copy.12
